TPU v7x, 32 devices: a whole 2x2x4 slice. The times are simulated.
32 devices in a mesh: groups: 2 (over x), pts: 16 (over z, y, core).
Axes of the slice: x: 2, y: 2, z: 4, core: 2. Of those that a mesh axis runs over, the one named last changes fastest.
Arguments:
- points: float32 [32, 8192], P(None, ('groups', 'pts')), parts along dimension 1, may hold values from -6 to 6
- lengthscales: float32 [32], replicated, may hold values from 1.4 to 3
- noise: float32 [8192], P(('groups', 'pts')), parts along dimension 0, may hold values from 0.2 to 1
- targets: float32 [32, 8192], P(None, ('groups', 'pts')), parts along dimension 1, may hold values from -6 to 6
Outputs:
- solution: float32 [32, 8192], P(None, ('groups', 'pts')), parts along dimension 1
- residual: float32 [32, 8192], P(None, ('groups', 'pts')), parts along dimension 1
There are 2 independent parts, one for each index of `groups`. A program takes and returns all parts, laid end to end along the dimension named above; an argument that names none is the same for every part. Nothing has to cross between parts.
All inputs are finite; a program needn't handle non-finite values.
Results may differ from a plain program's by a relative error of at most 0.0045.
Values sent between devices are 32-bit elements; how exact they have to be, the bound alone decides.
A program may use at most 64 MiB of HBM per device.

v0:
```python
import math
import jax
import jax.numpy as jnp
from jax import lax
from jax.sharding import PartitionSpec as P

ITERS = 3
root_five = math.sqrt(5.0)


def matern(left, right):
    cross = jnp.dot(
        left.T, right, precision=lax.Precision.HIGHEST, preferred_element_type=jnp.float32
    )
    dist2 = (
        jnp.sum(left * left, axis=0)[:, None]
        + jnp.sum(right * right, axis=0)[None, :]
        - 2.0 * cross
    )
    scaled_dist = root_five * jnp.sqrt(jnp.maximum(dist2, 0.0))
    return (1.0 + scaled_dist + scaled_dist * scaled_dist / 3.0) * jnp.exp(-scaled_dist)


def gram(left, right):
    return lax.dot_general(
        left,
        right,
        (((1,), (1,)), ((), ())),
        precision=lax.Precision.HIGHEST,
        preferred_element_type=jnp.float32,
    )


def symmetric(matrix):
    return 0.5 * (matrix + matrix.T)


def spd_solve(matrix, right):
    lower = jnp.linalg.cholesky(matrix)
    return jax.scipy.linalg.cho_solve((lower, True), right)


def product(left, right):
    return jnp.dot(left, right, precision=lax.Precision.HIGHEST, preferred_element_type=jnp.float32)


def accumulate(total, feat_piece, dir_piece, own):
    width = feat_piece.shape[1]
    block_cols = 256

    def one_block(index, carry):
        begin = index * block_cols
        feats = lax.dynamic_slice_in_dim(feat_piece, begin, block_cols, 1)
        dirs = lax.dynamic_slice_in_dim(dir_piece, begin, block_cols, 1)
        return carry + product(dirs, matern(feats, own))

    return lax.fori_loop(0, width // block_cols, one_block, total)


def residual_norm(residual):
    return symmetric(lax.psum(gram(residual, residual), "pts"))


def body(points, lengthscales, noise, targets):
    scaled = points / lengthscales[:, None]
    solution = jnp.zeros_like(targets)
    residual = targets
    direction = targets
    norm_now = residual_norm(residual)
    for step in range(ITERS):
        empty = jnp.zeros(direction.shape, jnp.float32)
        image = accumulate(
            empty,
            lax.all_gather(scaled, "pts", axis=1, tiled=True),
            lax.all_gather(direction, "pts", axis=1, tiled=True),
            scaled,
        )
        image = image + noise[None, :] * direction
        curv = symmetric(lax.psum(gram(direction, image), "pts"))
        alpha = spd_solve(curv, norm_now)
        solution = solution + product(alpha.T, direction)
        residual = residual - product(alpha.T, image)
        if step + 1 < ITERS:
            norm_next = residual_norm(residual)
        if step + 1 < ITERS:
            beta = spd_solve(norm_now, norm_next)
            direction = residual + product(beta.T, direction)
            norm_now = norm_next
    return (solution, residual)


def solution(mesh):
    placed = (P(None, ("groups", "pts")), P(), P(("groups", "pts")), P(None, ("groups", "pts")))
    return jax.shard_map(
        body,
        mesh=mesh,
        in_specs=placed,
        out_specs=(P(None, ("groups", "pts")), P(None, ("groups", "pts"))),
        check_vma=False,
    )
```

profile of v0, /device:TPU:0, one launch (start us, length us, event | category | flops | bytes accessed | tf_op | source)
XLA Modules:
  0.0 458.8 jit_solution(8361852773679806300)
XLA Ops:
  0.6 1.0 fusion.105
  1.7 24.6 %all_gather.14 = f32[32,4096]{1,0:T(8,128)S(1)} all-gather(f32[32,256]{1,0:T(8,128)S(1)} %copy-done), channel_id=1, replica_groups=mesh['groups'=2,'pts'=16] {'pts'}, dimensions={1}, use_global_device_ids=true | all-gather | bytes 557056 | tf_op jit(solution)/shard_map/all_gather | solution.py:75
  26.4 18.9 %all_gather.15 = f32[32,4096]{1,0:T(8,128)S(1)} all-gather(f32[32,256]{1,0:T(8,128)S(1)} %get-tuple-element.687), channel_id=1, replica_groups=mesh['groups'=2,'pts'=16] {'pts'}, dimensions={1}, use_global_device_ids=true | all-gather | bytes 557056 | tf_op jit(solution)/shard_map/all_gather | solution.py:74
  45.3 13.7 %while.48 = (s32[]{:T(128)}, f32[32,256]{1,0:T(8,128)S(1)}, f32[32,4096]{1,0:T(8,128)S(1)}, f32[32,4096]{1,0:T(8,128)S(1)}, f32[256]{0:T(256)S(1)}, /*index=5*/f...) while((s32[]{:T(128)}, f32[32,256]{1,0:T(8,128)S(1)}, ...), condition=%wide.region_3.4_spmd.clone, body=%wide.region_1.3_spmd.clone.sunk | while | flops 51085060 | bytes 724145 | solution.py:57
  47.0 0.5 fusion.161
  48.7 0.5 fusion.161
  49.6 0.5 fusion.161
  58.9 0.7 copy-done.1
  59.8 59.2 %all-reduce = (f32[32,32]{1,0:T(8,128)S(1)}, f32[32,32]{1,0:T(8,128)S(1)}) all-reduce(f32[32,32]{1,0:T(8,128)S(1)} %fusion.105, f32[32,32]{1,0:T(8,128)S(1)} %convolution_bitcast_fusion), channel_id=1, replica_groups=mesh['groups'=2,'pts'=16] {'pts'}, use_global_device_ids=true, to_apply=%region_7.9 | all-reduce | flops 2048 | bytes 16384 | tf_op jit(solution)/shard_map/psum | solution.py:61
  119.2 2.9 cholesky.89
  122.1 0.6 compare_reduce_fusion.4
  122.8 0.7 fusion.59
  123.4 2.4 custom-call.14
  126.9 57.6 %psum.44 = f32[32,32]{1,0:T(8,128)S(1)} all-reduce(f32[32,32]{1,0:T(8,128)S(1)} %fusion.107), channel_id=1, replica_groups=mesh['groups'=2,'pts'=16] {'pts'}, use_global_device_ids=true, to_apply=%region_8.11 | all-reduce | flops 1024 | bytes 8192 | tf_op jit(solution)/shard_map/psum | solution.py:61
  184.7 2.9 cholesky.100
  187.6 0.6 compare_reduce_fusion.3
  188.3 0.7 fusion.60
  188.9 2.4 custom-call.15
  192.0 18.7 %all_gather.16 = f32[32,4096]{1,0:T(8,128)S(1)} all-gather(f32[32,256]{1,0:T(8,128)S(1)} %convolution_add_fusion.6), channel_id=1, replica_groups=mesh['groups'=2,'pts'=16] {'pts'}, dimensions={1}, use_global_device_ids=true | all-gather | bytes 557056 | tf_op jit(solution)/shard_map/all_gather | solution.py:75
  210.7 13.7 %while.49 = (s32[]{:T(128)}, f32[32,256]{1,0:T(8,128)S(1)}, f32[32,4096]{1,0:T(8,128)S(1)}, f32[32,4096]{1,0:T(8,128)S(1)}, f32[256]{0:T(256)S(1)}, /*index=5*/f...) while((s32[]{:T(128)}, f32[32,256]{1,0:T(8,128)S(1)}, ...), condition=%wide.region_11.0_spmd.clone, body=%wide.region_9.13_spmd.clone.sunk | while | flops 51085060 | bytes 724145 | solution.py:57
  211.6 0.5 fusion.166
  212.4 0.5 fusion.166
  213.3 0.5 fusion.166
  215.0 0.5 fusion.166
  215.9 0.5 fusion.166
  218.4 0.5 fusion.166
  219.3 0.5 fusion.166
  221.9 0.5 fusion.166
  222.7 0.5 fusion.166
  224.6 59.8 %psum.45 = f32[32,32]{1,0:T(8,128)S(1)} all-reduce(f32[32,32]{1,0:T(8,128)S(1)} %fusion.57), channel_id=1, replica_groups=mesh['groups'=2,'pts'=16] {'pts'}, use_global_device_ids=true, to_apply=%region_12.0 | all-reduce | flops 1024 | bytes 8192 | tf_op jit(solution)/shard_map/psum | solution.py:79
  284.6 2.9 cholesky.111
  287.5 0.6 compare_reduce_fusion.2
  288.2 0.7 fusion.61
  288.8 2.4 custom-call.16
  292.2 2.9 cholesky.122
  295.2 0.6 compare_reduce_fusion.1
  295.8 0.7 fusion.62
  296.5 2.4 custom-call.17
  299.1 57.7 %psum.46 = f32[32,32]{1,0:T(8,128)S(1)} all-reduce(f32[32,32]{1,0:T(8,128)S(1)} %fusion.108), channel_id=1, replica_groups=mesh['groups'=2,'pts'=16] {'pts'}, use_global_device_ids=true, to_apply=%region_13.16 | all-reduce | flops 1024 | bytes 8192 | tf_op jit(solution)/shard_map/psum | solution.py:61
  357.5 18.7 %all_gather.17 = f32[32,4096]{1,0:T(8,128)S(1)} all-gather(f32[32,256]{1,0:T(8,128)S(1)} %convolution_add_fusion.4), channel_id=1, replica_groups=mesh['groups'=2,'pts'=16] {'pts'}, dimensions={1}, use_global_device_ids=true | all-gather | bytes 557056 | tf_op jit(solution)/shard_map/all_gather | solution.py:75
  376.2 13.7 %while.50 = (s32[]{:T(128)}, f32[32,256]{1,0:T(8,128)S(1)}, f32[32,4096]{1,0:T(8,128)S(1)}, f32[32,4096]{1,0:T(8,128)S(1)}, f32[256]{0:T(256)S(1)}, /*index=5*/f...) while((s32[]{:T(128)}, f32[32,256]{1,0:T(8,128)S(1)}, ...), condition=%wide.region_16.0_spmd.clone, body=%wide.region_14.18_spmd.clone.sunk | while | flops 51085060 | bytes 724145 | solution.py:57
  390.0 59.9 %psum.47 = f32[32,32]{1,0:T(8,128)S(1)} all-reduce(f32[32,32]{1,0:T(8,128)S(1)} %fusion.58), channel_id=1, replica_groups=mesh['groups'=2,'pts'=16] {'pts'}, use_global_device_ids=true, to_apply=%region_17.0 | all-reduce | flops 1024 | bytes 8192 | tf_op jit(solution)/shard_map/psum | solution.py:79
  450.1 2.9 cholesky.133
  453.0 0.6 compare_reduce_fusion
  453.7 0.7 fusion.63
  454.3 2.4 custom-call.18
  457.1 0.9 convolution_add_fusion.3
  458.0 0.8 convolution_subtract_fusion
  (189 shorter events, 38.4 us)
Async XLA Ops:
  0.6 1.0 copy-start
  1.7 24.6 %copy-start.2 = (f32[32,256]{1,0:T(8,128)S(1)}, f32[32,256]{1,0:T(8,128)}, u32[]{:S(2)}) copy-start(f32[32,256]{1,0:T(8,128)} %param.13) | copy-start | bytes 98308
  1.7 24.6 %copy-start.3 = (f32[32]{0:T(128)S(1)}, f32[32]{0:T(128)}, u32[]{:S(2)}) copy-start(f32[32]{0:T(128)} %param.14) | copy-start | bytes 388
  58.9 0.7 copy-start.1
where the time goes:
time: 459 us
  blocking collectives  375 us (82%)
  matrix products  44.7 us (10%)
  other arithmetic  34.9 us (8%)
    psum x3, blocking collectives, residual_norm(): return symmetric(lax.psum(gram(residual, residual), 'pts'))  174 us
    psum x2, blocking collectives, body(): curv = symmetric(lax.psum(gram(direction, image), 'pts'))  120 us
    all_gather x3, blocking collectives, body(): lax.all_gather(direction, 'pts', axis=1, tiled=True)  62 us
    dot_general x48, matrix products, matern(): jnp.dot(left.T, right, precision=lax.Precision.HIGHEST, preferred_element...  23.6 us
    all_gather x1, blocking collectives, body(): lax.all_gather(scaled, 'pts', axis=1, tiled=True)  18.9 us
    another operation x15, other arithmetic, spd_solve(): lower = jnp.linalg.cholesky(matrix)  18 us
    dot_general x56, matrix products, product(): jnp.dot(left, right, precision=lax.Precision.HIGHEST, preferred_element_t...  17.4 us
    another operation x10, other arithmetic, spd_solve(): return jax.scipy.linalg.cho_solve((lower, True), right)  15.4 us

commit v1 on v0

--- a/solution.py
+++ b/solution.py
@@ -6,6 +6,24 @@
 
 ITERS = 3
 root_five = math.sqrt(5.0)
+
+
+def collect(array, axis, dim):
+    ways, here, lap = (lax.axis_size(axis), lax.axis_index(axis), array.shape[dim])
+    shape = [n * ways if d == dim else n for d, n in enumerate(array.shape)]
+    full = lax.dynamic_update_slice_in_dim(
+        jnp.zeros(shape, array.dtype), array, here * lap, axis=dim
+    )
+    going_up = going_down = array
+    for far in range(1, ways // 2 + 1):
+        going_up = lax.ppermute(going_up, axis, [(d, (d + 1) % ways) for d in range(ways)])
+        full = lax.dynamic_update_slice_in_dim(full, going_up, (here - far) % ways * lap, axis=dim)
+        if 2 * far < ways:
+            going_down = lax.ppermute(going_down, axis, [(d, (d - 1) % ways) for d in range(ways)])
+            full = lax.dynamic_update_slice_in_dim(
+                full, going_down, (here + far) % ways * lap, axis=dim
+            )
+    return full
 
 
 def matern(left, right):
@@ -72,7 +90,7 @@
         image = accumulate(
             empty,
             lax.all_gather(scaled, "pts", axis=1, tiled=True),
-            lax.all_gather(direction, "pts", axis=1, tiled=True),
+            collect(direction, "pts", 1),
             scaled,
         )
         image = image + noise[None, :] * direction

time: 459 us -> 537 us (1.17)
  starting transfers between devices: 0 us -> 94.6 us
  blocking collectives: 375 us -> 309 us
  waiting for transfers between devices: 0 us -> 47.8 us
    ppermute x0 -> x45, starting transfers between devices: none -> 94.6 us  [the longest x21 93.5 us: collect(): lax.ppermute(going_down, axis, [(d, (d - 1) % ways) for d in range(ways)])]
    all_gather x3 -> x0, blocking collectives: 62 us -> none  [body(): lax.all_gather(direction, 'pts', axis=1, tiled=True)]
    ppermute x0 -> x45, waiting for transfers between devices: none -> 47.8 us  [the longest x24 47.2 us: collect(): lax.ppermute(going_up, axis, [(d, (d + 1) % ways) for d in range(ways)])]
  transfers between devices with their start and end apart: 0 -> 45, of which waited for: 0 -> 22; matrix products, arithmetic and copies ran while one was open for 0% -> 2% of each run, Pallas kernels for 0% -> 0%
where the time goes in v1:
time: 537 us
  blocking collectives  309 us (58%)
  starting transfers between devices  94.6 us (18%)
  waiting for transfers between devices  47.8 us (9%)
  matrix products  44.6 us (8%)
  other arithmetic  34.9 us (6%)
    psum x3, blocking collectives, residual_norm(): return symmetric(lax.psum(gram(residual, residual), 'pts'))  173 us
    psum x2, blocking collectives, body(): curv = symmetric(lax.psum(gram(direction, image), 'pts'))  115 us
    ppermute x21, starting transfers between devices, collect(): lax.ppermute(going_down, axis, [(d, (d - 1) % ways) for d in range(ways)])  93.5 us
    ppermute x24, waiting for transfers between devices, collect(): lax.ppermute(going_up, axis, [(d, (d + 1) % ways) for d in range(ways)])  47.2 us
    dot_general x48, matrix products, matern(): jnp.dot(left.T, right, precision=lax.Precision.HIGHEST, preferred_element...  23.6 us
    all_gather x1, blocking collectives, body(): lax.all_gather(scaled, 'pts', axis=1, tiled=True)  20.8 us
    another operation x15, other arithmetic, spd_solve(): lower = jnp.linalg.cholesky(matrix)  18 us
    dot_general x56, matrix products, product(): jnp.dot(left, right, precision=lax.Precision.HIGHEST, preferred_element_t...  17.4 us
  transfers between devices with their start and end apart: 45, of which 22 were waited for; matrix products, arithmetic and copies ran while one was open for 2% of the time, Pallas kernels for 0%

profile of v1, /device:TPU:0, one launch (start us, length us, event | category | flops | bytes accessed | tf_op | source)
XLA Modules:
  0.0 536.9 jit_solution(991284667421184901)
XLA Ops:
  1.1 5.1 collective-permute-start.1
  7.9 20.8 %all_gather.2 = f32[32,4096]{1,0:T(8,128)S(1)} all-gather(f32[32,256]{1,0:T(8,128)S(1)} %get-tuple-element.691), channel_id=1, replica_groups=mesh['groups'=2,'pts'=16] {'pts'}, dimensions={1}, use_global_device_ids=true | all-gather | bytes 557056 | tf_op jit(solution)/shard_map/all_gather | solution.py:92
  29.9 4.1 collective-permute-start.3
  34.0 1.6 collective-permute-done.2
  35.6 4.4 collective-permute-start.5
  40.0 1.6 collective-permute-done.4
  41.6 4.4 collective-permute-start.7
  46.1 1.6 collective-permute-done.6
  47.6 4.4 collective-permute-start.9
  52.1 1.6 collective-permute-done.8
  53.7 4.4 collective-permute-start.11
  58.1 1.6 collective-permute-done.10
  59.7 4.4 collective-permute-start.13
  65.8 6.0 %collective-permute-done.14 = f32[32,256]{1,0:T(8,128)S(1)} collective-permute-done((f32[32,256]{1,0:T(8,128)S(1)}, f32[32,256]{1,0:T(8,128)S(1)}, u32[]{:S(2)}, u32[]{:S(2)}) %collective-permute-start.14) | collective-permute-done | bytes 32800 | tf_op jit(solution)/shard_map/ppermute | solution.py:19
  71.8 13.7 %while.48 = (s32[]{:T(128)}, f32[32,256]{1,0:T(8,128)S(1)}, f32[32,4096]{1,0:T(8,128)S(1)}, f32[32,4096]{1,0:T(8,128)S(1)}, f32[256]{0:T(256)S(1)}, /*index=5*/f...) while((s32[]{:T(128)}, f32[32,256]{1,0:T(8,128)S(1)}, ...), condition=%wide.region_3.4_spmd.clone, body=%wide.region_1.3_spmd.clone.sunk | while | flops 51085060 | bytes 724137 | solution.py:75
  86.3 57.6 %all-reduce = (f32[32,32]{1,0:T(8,128)S(1)}, f32[32,32]{1,0:T(8,128)S(1)}) all-reduce(f32[32,32]{1,0:T(8,128)S(1)} %fusion.105, f32[32,32]{1,0:T(8,128)S(1)} %convolution_bitcast_fusion), channel_id=1, replica_groups=mesh['groups'=2,'pts'=16] {'pts'}, use_global_device_ids=true, to_apply=%region_7.9 | all-reduce | flops 2048 | bytes 16384 | tf_op jit(solution)/shard_map/psum | solution.py:79
  144.2 2.9 cholesky.89
  148.5 2.4 custom-call.14
  151.8 57.6 %psum.44 = f32[32,32]{1,0:T(8,128)S(1)} all-reduce(f32[32,32]{1,0:T(8,128)S(1)} %fusion.107), channel_id=1, replica_groups=mesh['groups'=2,'pts'=16] {'pts'}, use_global_device_ids=true, to_apply=%region_8.11 | all-reduce | flops 1024 | bytes 8192 | tf_op jit(solution)/shard_map/psum | solution.py:79
  209.6 2.9 cholesky.100
  213.8 2.4 custom-call.15
  217.0 4.4 collective-permute-start.16
  221.7 2.9 cholesky.122
  225.9 2.4 custom-call.17
  228.4 4.5 collective-permute-start.18
  234.5 4.4 collective-permute-start.20
  240.5 4.4 collective-permute-start.22
  246.5 4.4 collective-permute-start.24
  252.6 4.4 collective-permute-start.26
  258.6 4.4 collective-permute-start.28
  264.7 6.0 %collective-permute-done.29 = f32[32,256]{1,0:T(8,128)S(1)} collective-permute-done((f32[32,256]{1,0:T(8,128)S(1)}, f32[32,256]{1,0:T(8,128)S(1)}, u32[]{:S(2)}, u32[]{:S(2)}) %collective-permute-start.29) | collective-permute-done | bytes 32800 | tf_op jit(solution)/shard_map/ppermute | solution.py:19
  270.6 13.7 %while.49 = (s32[]{:T(128)}, f32[32,256]{1,0:T(8,128)S(1)}, f32[32,4096]{1,0:T(8,128)S(1)}, f32[32,4096]{1,0:T(8,128)S(1)}, f32[256]{0:T(256)S(1)}, /*index=5*/f...) while((s32[]{:T(128)}, f32[32,256]{1,0:T(8,128)S(1)}, ...), condition=%wide.region_11.14_spmd.clone, body=%wide.region_9.0_spmd.clone.sunk | while | flops 51085060 | bytes 724137 | solution.py:75
  284.5 57.6 %psum.45 = f32[32,32]{1,0:T(8,128)S(1)} all-reduce(f32[32,32]{1,0:T(8,128)S(1)} %fusion.57), channel_id=1, replica_groups=mesh['groups'=2,'pts'=16] {'pts'}, use_global_device_ids=true, to_apply=%region_12.15 | all-reduce | flops 1024 | bytes 8192 | tf_op jit(solution)/shard_map/psum | solution.py:97
  342.3 2.9 cholesky.111
  346.5 2.4 custom-call.16
  349.8 57.6 %psum.46 = f32[32,32]{1,0:T(8,128)S(1)} all-reduce(f32[32,32]{1,0:T(8,128)S(1)} %fusion.108), channel_id=1, replica_groups=mesh['groups'=2,'pts'=16] {'pts'}, use_global_device_ids=true, to_apply=%region_13.16 | all-reduce | flops 1024 | bytes 8192 | tf_op jit(solution)/shard_map/psum | solution.py:79
  408.2 4.4 collective-permute-start.31
  414.2 4.5 collective-permute-start.33
  420.3 4.4 collective-permute-start.35
  426.3 4.4 collective-permute-start.37
  432.4 4.4 collective-permute-start.39
  438.4 4.4 collective-permute-start.41
  444.4 4.4 collective-permute-start.43
  450.5 6.0 %collective-permute-done.44 = f32[32,256]{1,0:T(8,128)S(1)} collective-permute-done((f32[32,256]{1,0:T(8,128)S(1)}, f32[32,256]{1,0:T(8,128)S(1)}, u32[]{:S(2)}, u32[]{:S(2)}) %collective-permute-start.44) | collective-permute-done | bytes 32800 | tf_op jit(solution)/shard_map/ppermute | solution.py:19
  456.5 13.7 %while.50 = (s32[]{:T(128)}, f32[32,256]{1,0:T(8,128)S(1)}, f32[32,4096]{1,0:T(8,128)S(1)}, f32[32,4096]{1,0:T(8,128)S(1)}, f32[256]{0:T(256)S(1)}, /*index=5*/f...) while((s32[]{:T(128)}, f32[32,256]{1,0:T(8,128)S(1)}, ...), condition=%wide.region_16.19_spmd.clone, body=%wide.region_14.0_spmd.clone.sunk | while | flops 51085060 | bytes 724137 | solution.py:75
  470.3 57.6 %psum.47 = f32[32,32]{1,0:T(8,128)S(1)} all-reduce(f32[32,32]{1,0:T(8,128)S(1)} %fusion.58), channel_id=1, replica_groups=mesh['groups'=2,'pts'=16] {'pts'}, use_global_device_ids=true, to_apply=%region_17.20 | all-reduce | flops 1024 | bytes 8192 | tf_op jit(solution)/shard_map/psum | solution.py:97
  528.1 2.9 cholesky.133
  532.4 2.4 custom-call.18
  (325 shorter events, 78.9 us)
Async XLA Ops:
  0.6 28.8 %collective-permute-start = (f32[32,256]{1,0:T(8,128)}, f32[32,256]{1,0:T(8,128)S(1)}, u32[]{:S(2)}, u32[]{:S(2)}) collective-permute-start(f32[32,256]{1,0:T(8,128)} %param.16), channel_id=1, source_target_pairs={{0,1},{1,2},{2,3},{3,4},{4,5},{5,6},{6,7},{7,8},{8,9},{9,10},{10,1... | collective-permute-start | bytes 98312 | tf_op jit(solution)/shard_map/ppermute | solution.py:19
  1.1 28.7 %collective-permute-start.1 = (f32[32,256]{1,0:T(8,128)}, f32[32,256]{1,0:T(8,128)S(1)}, u32[]{:S(2)}, u32[]{:S(2)}) collective-permute-start(f32[32,256]{1,0:T(8,128)} %param.16), channel_id=1, source_target_pairs={{0,15},{1,0},{2,1},{3,2},{4,3},{5,4},{6,5},{7,6},{8,7},{9,8},{10,9... | collective-permute-start | bytes 98312 | tf_op jit(solution)/shard_map/ppermute | solution.py:22
  6.2 1.0 copy-start.2
  28.7 0.8 copy-start
  29.5 6.1 %collective-permute-start.2 = (f32[32,256]{1,0:T(8,128)S(1)}, f32[32,256]{1,0:T(8,128)S(1)}, u32[]{:S(2)}, u32[]{:S(2)}) collective-permute-start(f32[32,256]{1,0:T(8,128)S(1)} %collective-permute-done), channel_id=1, source_target_pairs={{0,1},{1,2},{2,3},{3,4},{4,5},{5,6},{6,7},{7,8},{8,9},{9,10},{10,1... | collective-permute-start | bytes 98312 | tf_op jit(solution)/shard_map/ppermute | solution.py:19
  29.9 5.7 %collective-permute-start.3 = (f32[32,256]{1,0:T(8,128)S(1)}, f32[32,256]{1,0:T(8,128)S(1)}, u32[]{:S(2)}, u32[]{:S(2)}) collective-permute-start(f32[32,256]{1,0:T(8,128)S(1)} %collective-permute-done.1), channel_id=1, source_target_pairs={{0,15},{1,0},{2,1},{3,2},{4,3},{5,4},{6,5},{7,6},{8,7},{9,8},{10,9... | collective-permute-start | bytes 98312 | tf_op jit(solution)/shard_map/ppermute | solution.py:22
  35.6 6.0 %collective-permute-start.4 = (f32[32,256]{1,0:T(8,128)S(1)}, f32[32,256]{1,0:T(8,128)S(1)}, u32[]{:S(2)}, u32[]{:S(2)}) collective-permute-start(f32[32,256]{1,0:T(8,128)S(1)} %collective-permute-done.2), channel_id=1, source_target_pairs={{0,1},{1,2},{2,3},{3,4},{4,5},{5,6},{6,7},{7,8},{8,9},{9,10},{10,1... | collective-permute-start | bytes 98312 | tf_op jit(solution)/shard_map/ppermute | solution.py:19
  35.6 6.0 %collective-permute-start.5 = (f32[32,256]{1,0:T(8,128)S(1)}, f32[32,256]{1,0:T(8,128)S(1)}, u32[]{:S(2)}, u32[]{:S(2)}) collective-permute-start(f32[32,256]{1,0:T(8,128)S(1)} %collective-permute-done.3), channel_id=1, source_target_pairs={{0,15},{1,0},{2,1},{3,2},{4,3},{5,4},{6,5},{7,6},{8,7},{9,8},{10,9... | collective-permute-start | bytes 98312 | tf_op jit(solution)/shard_map/ppermute | solution.py:22
  41.6 6.0 %collective-permute-start.6 = (f32[32,256]{1,0:T(8,128)S(1)}, f32[32,256]{1,0:T(8,128)S(1)}, u32[]{:S(2)}, u32[]{:S(2)}) collective-permute-start(f32[32,256]{1,0:T(8,128)S(1)} %collective-permute-done.4), channel_id=1, source_target_pairs={{0,1},{1,2},{2,3},{3,4},{4,5},{5,6},{6,7},{7,8},{8,9},{9,10},{10,1... | collective-permute-start | bytes 98312 | tf_op jit(solution)/shard_map/ppermute | solution.py:19
  41.6 6.0 %collective-permute-start.7 = (f32[32,256]{1,0:T(8,128)S(1)}, f32[32,256]{1,0:T(8,128)S(1)}, u32[]{:S(2)}, u32[]{:S(2)}) collective-permute-start(f32[32,256]{1,0:T(8,128)S(1)} %collective-permute-done.5), channel_id=1, source_target_pairs={{0,15},{1,0},{2,1},{3,2},{4,3},{5,4},{6,5},{7,6},{8,7},{9,8},{10,9... | collective-permute-start | bytes 98312 | tf_op jit(solution)/shard_map/ppermute | solution.py:22
  47.6 6.0 %collective-permute-start.8 = (f32[32,256]{1,0:T(8,128)S(1)}, f32[32,256]{1,0:T(8,128)S(1)}, u32[]{:S(2)}, u32[]{:S(2)}) collective-permute-start(f32[32,256]{1,0:T(8,128)S(1)} %collective-permute-done.6), channel_id=1, source_target_pairs={{0,1},{1,2},{2,3},{3,4},{4,5},{5,6},{6,7},{7,8},{8,9},{9,10},{10,1... | collective-permute-start | bytes 98312 | tf_op jit(solution)/shard_map/ppermute | solution.py:19
  47.6 6.0 %collective-permute-start.9 = (f32[32,256]{1,0:T(8,128)S(1)}, f32[32,256]{1,0:T(8,128)S(1)}, u32[]{:S(2)}, u32[]{:S(2)}) collective-permute-start(f32[32,256]{1,0:T(8,128)S(1)} %collective-permute-done.7), channel_id=1, source_target_pairs={{0,15},{1,0},{2,1},{3,2},{4,3},{5,4},{6,5},{7,6},{8,7},{9,8},{10,9... | collective-permute-start | bytes 98312 | tf_op jit(solution)/shard_map/ppermute | solution.py:22
  53.7 6.0 %collective-permute-start.10 = (f32[32,256]{1,0:T(8,128)S(1)}, f32[32,256]{1,0:T(8,128)S(1)}, u32[]{:S(2)}, u32[]{:S(2)}) collective-permute-start(f32[32,256]{1,0:T(8,128)S(1)} %collective-permute-done.8), channel_id=1, source_target_pairs={{0,1},{1,2},{2,3},{3,4},{4,5},{5,6},{6,7},{7,8},{8,9},{9,10},{10,1... | collective-permute-start | bytes 98312 | tf_op jit(solution)/shard_map/ppermute | solution.py:19
  53.7 6.0 %collective-permute-start.11 = (f32[32,256]{1,0:T(8,128)S(1)}, f32[32,256]{1,0:T(8,128)S(1)}, u32[]{:S(2)}, u32[]{:S(2)}) collective-permute-start(f32[32,256]{1,0:T(8,128)S(1)} %collective-permute-done.9), channel_id=1, source_target_pairs={{0,15},{1,0},{2,1},{3,2},{4,3},{5,4},{6,5},{7,6},{8,7},{9,8},{10,9... | collective-permute-start | bytes 98312 | tf_op jit(solution)/shard_map/ppermute | solution.py:22
  59.7 6.0 %collective-permute-start.12 = (f32[32,256]{1,0:T(8,128)S(1)}, f32[32,256]{1,0:T(8,128)S(1)}, u32[]{:S(2)}, u32[]{:S(2)}) collective-permute-start(f32[32,256]{1,0:T(8,128)S(1)} %collective-permute-done.10), channel_id=1, source_target_pairs={{0,1},{1,2},{2,3},{3,4},{4,5},{5,6},{6,7},{7,8},{8,9},{9,10},{10,1... | collective-permute-start | bytes 98312 | tf_op jit(solution)/shard_map/ppermute | solution.py:19
  59.7 6.0 %collective-permute-start.13 = (f32[32,256]{1,0:T(8,128)S(1)}, f32[32,256]{1,0:T(8,128)S(1)}, u32[]{:S(2)}, u32[]{:S(2)}) collective-permute-start(f32[32,256]{1,0:T(8,128)S(1)} %collective-permute-done.11), channel_id=1, source_target_pairs={{0,15},{1,0},{2,1},{3,2},{4,3},{5,4},{6,5},{7,6},{8,7},{9,8},{10,9... | collective-permute-start | bytes 98312 | tf_op jit(solution)/shard_map/ppermute | solution.py:22
  65.8 6.0 %collective-permute-start.14 = (f32[32,256]{1,0:T(8,128)S(1)}, f32[32,256]{1,0:T(8,128)S(1)}, u32[]{:S(2)}, u32[]{:S(2)}) collective-permute-start(f32[32,256]{1,0:T(8,128)S(1)} %collective-permute-done.12), channel_id=1, source_target_pairs={{0,1},{1,2},{2,3},{3,4},{4,5},{5,6},{6,7},{7,8},{8,9},{9,10},{10,1... | collective-permute-start | bytes 98312 | tf_op jit(solution)/shard_map/ppermute | solution.py:19
  85.5 0.7 copy-start.1
  216.9 11.4 %collective-permute-start.15 = (f32[32,256]{1,0:T(8,128)S(1)}, f32[32,256]{1,0:T(8,128)S(1)}, u32[]{:S(2)}, u32[]{:S(2)}) collective-permute-start(f32[32,256]{1,0:T(8,128)S(1)} %get-tuple-element.510), channel_id=1, source_target_pairs={{0,1},{1,2},{2,3},{3,4},{4,5},{5,6},{6,7},{7,8},{8,9},{9,10},{10,1... | collective-permute-start | bytes 98312 | tf_op jit(solution)/shard_map/ppermute | solution.py:19
  217.0 11.4 %collective-permute-start.16 = (f32[32,256]{1,0:T(8,128)S(1)}, f32[32,256]{1,0:T(8,128)S(1)}, u32[]{:S(2)}, u32[]{:S(2)}) collective-permute-start(f32[32,256]{1,0:T(8,128)S(1)} %get-tuple-element.510), channel_id=1, source_target_pairs={{0,15},{1,0},{2,1},{3,2},{4,3},{5,4},{6,5},{7,6},{8,7},{9,8},{10,9... | collective-permute-start | bytes 98312 | tf_op jit(solution)/shard_map/ppermute | solution.py:22
  228.3 6.1 %collective-permute-start.17 = (f32[32,256]{1,0:T(8,128)S(1)}, f32[32,256]{1,0:T(8,128)S(1)}, u32[]{:S(2)}, u32[]{:S(2)}) collective-permute-start(f32[32,256]{1,0:T(8,128)S(1)} %collective-permute-done.15), channel_id=1, source_target_pairs={{0,1},{1,2},{2,3},{3,4},{4,5},{5,6},{6,7},{7,8},{8,9},{9,10},{10,1... | collective-permute-start | bytes 98312 | tf_op jit(solution)/shard_map/ppermute | solution.py:19
  228.4 6.1 %collective-permute-start.18 = (f32[32,256]{1,0:T(8,128)S(1)}, f32[32,256]{1,0:T(8,128)S(1)}, u32[]{:S(2)}, u32[]{:S(2)}) collective-permute-start(f32[32,256]{1,0:T(8,128)S(1)} %collective-permute-done.16), channel_id=1, source_target_pairs={{0,15},{1,0},{2,1},{3,2},{4,3},{5,4},{6,5},{7,6},{8,7},{9,8},{10,9... | collective-permute-start | bytes 98312 | tf_op jit(solution)/shard_map/ppermute | solution.py:22
  234.4 6.0 %collective-permute-start.19 = (f32[32,256]{1,0:T(8,128)S(1)}, f32[32,256]{1,0:T(8,128)S(1)}, u32[]{:S(2)}, u32[]{:S(2)}) collective-permute-start(f32[32,256]{1,0:T(8,128)S(1)} %collective-permute-done.17), channel_id=1, source_target_pairs={{0,1},{1,2},{2,3},{3,4},{4,5},{5,6},{6,7},{7,8},{8,9},{9,10},{10,1... | collective-permute-start | bytes 98312 | tf_op jit(solution)/shard_map/ppermute | solution.py:19
  234.5 6.0 %collective-permute-start.20 = (f32[32,256]{1,0:T(8,128)S(1)}, f32[32,256]{1,0:T(8,128)S(1)}, u32[]{:S(2)}, u32[]{:S(2)}) collective-permute-start(f32[32,256]{1,0:T(8,128)S(1)} %collective-permute-done.18), channel_id=1, source_target_pairs={{0,15},{1,0},{2,1},{3,2},{4,3},{5,4},{6,5},{7,6},{8,7},{9,8},{10,9... | collective-permute-start | bytes 98312 | tf_op jit(solution)/shard_map/ppermute | solution.py:22
  240.4 6.0 %collective-permute-start.21 = (f32[32,256]{1,0:T(8,128)S(1)}, f32[32,256]{1,0:T(8,128)S(1)}, u32[]{:S(2)}, u32[]{:S(2)}) collective-permute-start(f32[32,256]{1,0:T(8,128)S(1)} %collective-permute-done.19), channel_id=1, source_target_pairs={{0,1},{1,2},{2,3},{3,4},{4,5},{5,6},{6,7},{7,8},{8,9},{9,10},{10,1... | collective-permute-start | bytes 98312 | tf_op jit(solution)/shard_map/ppermute | solution.py:19
  240.5 6.0 %collective-permute-start.22 = (f32[32,256]{1,0:T(8,128)S(1)}, f32[32,256]{1,0:T(8,128)S(1)}, u32[]{:S(2)}, u32[]{:S(2)}) collective-permute-start(f32[32,256]{1,0:T(8,128)S(1)} %collective-permute-done.20), channel_id=1, source_target_pairs={{0,15},{1,0},{2,1},{3,2},{4,3},{5,4},{6,5},{7,6},{8,7},{9,8},{10,9... | collective-permute-start | bytes 98312 | tf_op jit(solution)/shard_map/ppermute | solution.py:22
  246.5 6.0 %collective-permute-start.23 = (f32[32,256]{1,0:T(8,128)S(1)}, f32[32,256]{1,0:T(8,128)S(1)}, u32[]{:S(2)}, u32[]{:S(2)}) collective-permute-start(f32[32,256]{1,0:T(8,128)S(1)} %collective-permute-done.21), channel_id=1, source_target_pairs={{0,1},{1,2},{2,3},{3,4},{4,5},{5,6},{6,7},{7,8},{8,9},{9,10},{10,1... | collective-permute-start | bytes 98312 | tf_op jit(solution)/shard_map/ppermute | solution.py:19
  246.5 6.0 %collective-permute-start.24 = (f32[32,256]{1,0:T(8,128)S(1)}, f32[32,256]{1,0:T(8,128)S(1)}, u32[]{:S(2)}, u32[]{:S(2)}) collective-permute-start(f32[32,256]{1,0:T(8,128)S(1)} %collective-permute-done.22), channel_id=1, source_target_pairs={{0,15},{1,0},{2,1},{3,2},{4,3},{5,4},{6,5},{7,6},{8,7},{9,8},{10,9... | collective-permute-start | bytes 98312 | tf_op jit(solution)/shard_map/ppermute | solution.py:22
  252.5 6.0 %collective-permute-start.25 = (f32[32,256]{1,0:T(8,128)S(1)}, f32[32,256]{1,0:T(8,128)S(1)}, u32[]{:S(2)}, u32[]{:S(2)}) collective-permute-start(f32[32,256]{1,0:T(8,128)S(1)} %collective-permute-done.23), channel_id=1, source_target_pairs={{0,1},{1,2},{2,3},{3,4},{4,5},{5,6},{6,7},{7,8},{8,9},{9,10},{10,1... | collective-permute-start | bytes 98312 | tf_op jit(solution)/shard_map/ppermute | solution.py:19
  252.6 6.0 %collective-permute-start.26 = (f32[32,256]{1,0:T(8,128)S(1)}, f32[32,256]{1,0:T(8,128)S(1)}, u32[]{:S(2)}, u32[]{:S(2)}) collective-permute-start(f32[32,256]{1,0:T(8,128)S(1)} %collective-permute-done.24), channel_id=1, source_target_pairs={{0,15},{1,0},{2,1},{3,2},{4,3},{5,4},{6,5},{7,6},{8,7},{9,8},{10,9... | collective-permute-start | bytes 98312 | tf_op jit(solution)/shard_map/ppermute | solution.py:22
  258.6 6.0 %collective-permute-start.27 = (f32[32,256]{1,0:T(8,128)S(1)}, f32[32,256]{1,0:T(8,128)S(1)}, u32[]{:S(2)}, u32[]{:S(2)}) collective-permute-start(f32[32,256]{1,0:T(8,128)S(1)} %collective-permute-done.25), channel_id=1, source_target_pairs={{0,1},{1,2},{2,3},{3,4},{4,5},{5,6},{6,7},{7,8},{8,9},{9,10},{10,1... | collective-permute-start | bytes 98312 | tf_op jit(solution)/shard_map/ppermute | solution.py:19
  258.6 6.0 %collective-permute-start.28 = (f32[32,256]{1,0:T(8,128)S(1)}, f32[32,256]{1,0:T(8,128)S(1)}, u32[]{:S(2)}, u32[]{:S(2)}) collective-permute-start(f32[32,256]{1,0:T(8,128)S(1)} %collective-permute-done.26), channel_id=1, source_target_pairs={{0,15},{1,0},{2,1},{3,2},{4,3},{5,4},{6,5},{7,6},{8,7},{9,8},{10,9... | collective-permute-start | bytes 98312 | tf_op jit(solution)/shard_map/ppermute | solution.py:22
  264.6 6.0 %collective-permute-start.29 = (f32[32,256]{1,0:T(8,128)S(1)}, f32[32,256]{1,0:T(8,128)S(1)}, u32[]{:S(2)}, u32[]{:S(2)}) collective-permute-start(f32[32,256]{1,0:T(8,128)S(1)} %collective-permute-done.27), channel_id=1, source_target_pairs={{0,1},{1,2},{2,3},{3,4},{4,5},{5,6},{6,7},{7,8},{8,9},{9,10},{10,1... | collective-permute-start | bytes 98312 | tf_op jit(solution)/shard_map/ppermute | solution.py:19
  408.1 6.1 %collective-permute-start.30 = (f32[32,256]{1,0:T(8,128)S(1)}, f32[32,256]{1,0:T(8,128)S(1)}, u32[]{:S(2)}, u32[]{:S(2)}) collective-permute-start(f32[32,256]{1,0:T(8,128)S(1)} %get-tuple-element.512), channel_id=1, source_target_pairs={{0,1},{1,2},{2,3},{3,4},{4,5},{5,6},{6,7},{7,8},{8,9},{9,10},{10,1... | collective-permute-start | bytes 98312 | tf_op jit(solution)/shard_map/ppermute | solution.py:19
  408.2 6.0 %collective-permute-start.31 = (f32[32,256]{1,0:T(8,128)S(1)}, f32[32,256]{1,0:T(8,128)S(1)}, u32[]{:S(2)}, u32[]{:S(2)}) collective-permute-start(f32[32,256]{1,0:T(8,128)S(1)} %get-tuple-element.512), channel_id=1, source_target_pairs={{0,15},{1,0},{2,1},{3,2},{4,3},{5,4},{6,5},{7,6},{8,7},{9,8},{10,9... | collective-permute-start | bytes 98312 | tf_op jit(solution)/shard_map/ppermute | solution.py:22
  414.2 6.0 %collective-permute-start.32 = (f32[32,256]{1,0:T(8,128)S(1)}, f32[32,256]{1,0:T(8,128)S(1)}, u32[]{:S(2)}, u32[]{:S(2)}) collective-permute-start(f32[32,256]{1,0:T(8,128)S(1)} %collective-permute-done.30), channel_id=1, source_target_pairs={{0,1},{1,2},{2,3},{3,4},{4,5},{5,6},{6,7},{7,8},{8,9},{9,10},{10,1... | collective-permute-start | bytes 98312 | tf_op jit(solution)/shard_map/ppermute | solution.py:19
  414.2 6.1 %collective-permute-start.33 = (f32[32,256]{1,0:T(8,128)S(1)}, f32[32,256]{1,0:T(8,128)S(1)}, u32[]{:S(2)}, u32[]{:S(2)}) collective-permute-start(f32[32,256]{1,0:T(8,128)S(1)} %collective-permute-done.31), channel_id=1, source_target_pairs={{0,15},{1,0},{2,1},{3,2},{4,3},{5,4},{6,5},{7,6},{8,7},{9,8},{10,9... | collective-permute-start | bytes 98312 | tf_op jit(solution)/shard_map/ppermute | solution.py:22
  420.2 6.0 %collective-permute-start.34 = (f32[32,256]{1,0:T(8,128)S(1)}, f32[32,256]{1,0:T(8,128)S(1)}, u32[]{:S(2)}, u32[]{:S(2)}) collective-permute-start(f32[32,256]{1,0:T(8,128)S(1)} %collective-permute-done.32), channel_id=1, source_target_pairs={{0,1},{1,2},{2,3},{3,4},{4,5},{5,6},{6,7},{7,8},{8,9},{9,10},{10,1... | collective-permute-start | bytes 98312 | tf_op jit(solution)/shard_map/ppermute | solution.py:19
  420.3 6.0 %collective-permute-start.35 = (f32[32,256]{1,0:T(8,128)S(1)}, f32[32,256]{1,0:T(8,128)S(1)}, u32[]{:S(2)}, u32[]{:S(2)}) collective-permute-start(f32[32,256]{1,0:T(8,128)S(1)} %collective-permute-done.33), channel_id=1, source_target_pairs={{0,15},{1,0},{2,1},{3,2},{4,3},{5,4},{6,5},{7,6},{8,7},{9,8},{10,9... | collective-permute-start | bytes 98312 | tf_op jit(solution)/shard_map/ppermute | solution.py:22
  426.3 6.0 %collective-permute-start.36 = (f32[32,256]{1,0:T(8,128)S(1)}, f32[32,256]{1,0:T(8,128)S(1)}, u32[]{:S(2)}, u32[]{:S(2)}) collective-permute-start(f32[32,256]{1,0:T(8,128)S(1)} %collective-permute-done.34), channel_id=1, source_target_pairs={{0,1},{1,2},{2,3},{3,4},{4,5},{5,6},{6,7},{7,8},{8,9},{9,10},{10,1... | collective-permute-start | bytes 98312 | tf_op jit(solution)/shard_map/ppermute | solution.py:19
  426.3 6.0 %collective-permute-start.37 = (f32[32,256]{1,0:T(8,128)S(1)}, f32[32,256]{1,0:T(8,128)S(1)}, u32[]{:S(2)}, u32[]{:S(2)}) collective-permute-start(f32[32,256]{1,0:T(8,128)S(1)} %collective-permute-done.35), channel_id=1, source_target_pairs={{0,15},{1,0},{2,1},{3,2},{4,3},{5,4},{6,5},{7,6},{8,7},{9,8},{10,9... | collective-permute-start | bytes 98312 | tf_op jit(solution)/shard_map/ppermute | solution.py:22
  432.3 6.0 %collective-permute-start.38 = (f32[32,256]{1,0:T(8,128)S(1)}, f32[32,256]{1,0:T(8,128)S(1)}, u32[]{:S(2)}, u32[]{:S(2)}) collective-permute-start(f32[32,256]{1,0:T(8,128)S(1)} %collective-permute-done.36), channel_id=1, source_target_pairs={{0,1},{1,2},{2,3},{3,4},{4,5},{5,6},{6,7},{7,8},{8,9},{9,10},{10,1... | collective-permute-start | bytes 98312 | tf_op jit(solution)/shard_map/ppermute | solution.py:19
  432.4 6.0 %collective-permute-start.39 = (f32[32,256]{1,0:T(8,128)S(1)}, f32[32,256]{1,0:T(8,128)S(1)}, u32[]{:S(2)}, u32[]{:S(2)}) collective-permute-start(f32[32,256]{1,0:T(8,128)S(1)} %collective-permute-done.37), channel_id=1, source_target_pairs={{0,15},{1,0},{2,1},{3,2},{4,3},{5,4},{6,5},{7,6},{8,7},{9,8},{10,9... | collective-permute-start | bytes 98312 | tf_op jit(solution)/shard_map/ppermute | solution.py:22
  438.3 6.0 %collective-permute-start.40 = (f32[32,256]{1,0:T(8,128)S(1)}, f32[32,256]{1,0:T(8,128)S(1)}, u32[]{:S(2)}, u32[]{:S(2)}) collective-permute-start(f32[32,256]{1,0:T(8,128)S(1)} %collective-permute-done.38), channel_id=1, source_target_pairs={{0,1},{1,2},{2,3},{3,4},{4,5},{5,6},{6,7},{7,8},{8,9},{9,10},{10,1... | collective-permute-start | bytes 98312 | tf_op jit(solution)/shard_map/ppermute | solution.py:19
  438.4 6.0 %collective-permute-start.41 = (f32[32,256]{1,0:T(8,128)S(1)}, f32[32,256]{1,0:T(8,128)S(1)}, u32[]{:S(2)}, u32[]{:S(2)}) collective-permute-start(f32[32,256]{1,0:T(8,128)S(1)} %collective-permute-done.39), channel_id=1, source_target_pairs={{0,15},{1,0},{2,1},{3,2},{4,3},{5,4},{6,5},{7,6},{8,7},{9,8},{10,9... | collective-permute-start | bytes 98312 | tf_op jit(solution)/shard_map/ppermute | solution.py:22
  444.4 6.0 %collective-permute-start.42 = (f32[32,256]{1,0:T(8,128)S(1)}, f32[32,256]{1,0:T(8,128)S(1)}, u32[]{:S(2)}, u32[]{:S(2)}) collective-permute-start(f32[32,256]{1,0:T(8,128)S(1)} %collective-permute-done.40), channel_id=1, source_target_pairs={{0,1},{1,2},{2,3},{3,4},{4,5},{5,6},{6,7},{7,8},{8,9},{9,10},{10,1... | collective-permute-start | bytes 98312 | tf_op jit(solution)/shard_map/ppermute | solution.py:19
  444.4 6.0 %collective-permute-start.43 = (f32[32,256]{1,0:T(8,128)S(1)}, f32[32,256]{1,0:T(8,128)S(1)}, u32[]{:S(2)}, u32[]{:S(2)}) collective-permute-start(f32[32,256]{1,0:T(8,128)S(1)} %collective-permute-done.41), channel_id=1, source_target_pairs={{0,15},{1,0},{2,1},{3,2},{4,3},{5,4},{6,5},{7,6},{8,7},{9,8},{10,9... | collective-permute-start | bytes 98312 | tf_op jit(solution)/shard_map/ppermute | solution.py:22
  450.4 6.0 %collective-permute-start.44 = (f32[32,256]{1,0:T(8,128)S(1)}, f32[32,256]{1,0:T(8,128)S(1)}, u32[]{:S(2)}, u32[]{:S(2)}) collective-permute-start(f32[32,256]{1,0:T(8,128)S(1)} %collective-permute-done.42), channel_id=1, source_target_pairs={{0,1},{1,2},{2,3},{3,4},{4,5},{5,6},{6,7},{7,8},{8,9},{9,10},{10,1... | collective-permute-start | bytes 98312 | tf_op jit(solution)/shard_map/ppermute | solution.py:19
  (1 other events, 0.7 us)
